TPU v7x, 32 devices: a whole 2x2x4 slice. The times are simulated.
32 devices in a mesh: lat: 8 (over y, x, core), chan: 4 (over z).
Axes of the slice: x: 2, y: 2, z: 4, core: 2. Of those that a mesh axis runs over, the one named last changes fastest.
Arguments:
- signal: bfloat16 [384, 384, 1440], P('lat', 'chan'), may hold values from -6 to 6
- spectral_filter: float32 [384, 2, 384], replicated, may hold values from -4 to 4
- channel_mix: bfloat16 [2, 384, 384], replicated, may hold values from -0.21875 to 0.21875
Outputs:
- output: bfloat16 [384, 384, 1440], P('lat', 'chan')
All inputs are finite; a program needn't handle non-finite values.
Results may differ from a plain program's by a relative error of at most 0.01.
Values may be sent and summed in bfloat16 or wider, within the bound.
No kernel may reach another device: no remote copies, remote signals or barrier semaphores. Data moves between devices by JAX's collectives and lax.ppermute only.
A program may use at most 192 MiB of HBM per device.

v0:
```python
import math
import jax
import jax.numpy as jnp
from jax import lax
from jax.sharding import PartitionSpec as P

LB = 128


def fourier_tables(orders, lon_count):
    cells = jnp.arange(lon_count, dtype=jnp.int32)
    phase = orders[:, None] * cells[None, :] % lon_count
    angle = phase.astype(jnp.float32) * (2.0 * math.pi / lon_count)
    forward = jnp.stack([jnp.cos(angle), -jnp.sin(angle)], 0)
    factor = jnp.where(orders == 0, 1.0, 2.0).astype(jnp.float32)[None, :, None]
    return (forward.astype(jnp.bfloat16), (forward * factor).astype(jnp.bfloat16))


def latitude_terms(lat_index, lat_total, lon_count):
    theta = (lat_index.astype(jnp.float32) + 0.5) * (math.pi / lat_total)
    weight = jnp.sin(theta) * (2.0 * math.pi * math.pi / (lat_total * lon_count))
    return (jnp.cos(theta), jnp.log(jnp.sin(theta)), weight)


def seed_logs(orders, log_sine):
    order_f = orders.astype(jnp.float32)[:, None]
    base_term = 0.5 * jnp.log((2.0 * order_f + 1.0) / (4.0 * math.pi))
    ratio_term = 0.5 * (
        jax.scipy.special.gammaln(order_f + 0.5)
        - jax.scipy.special.gammaln(order_f + 1.0)
        - 0.5 * math.log(math.pi)
    )
    return base_term + ratio_term + order_f * log_sine[None, :]


def legendre_rows(recursion, orders, log_seeds, first_degree, row_count, cosine):
    order_f = orders.astype(jnp.float32)[:, None]

    def advance(carried, degree):
        previous, earlier, log_scale = carried
        degree_f = degree.astype(jnp.float32)
        degree_gap = degree_f * degree_f - order_f * order_f
        coeff_a = jnp.sqrt((4.0 * degree_f * degree_f - 1.0) / jnp.maximum(degree_gap, 1.0))
        below_sq = (degree_f - 1.0) * (degree_f - 1.0)
        coeff_b = jnp.sqrt(jnp.maximum(below_sq - order_f * order_f, 0.0) / (4.0 * below_sq - 1.0))
        grown = coeff_a * (cosine[None, :] * previous - coeff_b * earlier)
        at_start = degree_f == order_f
        is_above = degree_f > order_f
        fresh_value = jnp.where(at_start, 1.0, jnp.where(is_above, grown, 0.0))
        log_scale = jnp.where(at_start, log_seeds, log_scale)
        scaled_value = fresh_value * jnp.exp(log_scale)
        rescale = jnp.where(degree_f >= order_f, jnp.abs(fresh_value) + jnp.abs(previous), 1.0)
        return (
            (fresh_value / rescale, previous / rescale, log_scale + jnp.log(rescale)),
            scaled_value,
        )

    degrees_here = first_degree + jnp.arange(row_count, dtype=jnp.int32)
    carried, values = lax.scan(advance, recursion, degrees_here, unroll=8)
    return (carried, jnp.moveaxis(values, 0, 1))


def apply_filter(coefficients, gains):
    real_part = coefficients[..., 0, :] * gains[:, 0, :] - coefficients[..., 1, :] * gains[:, 1, :]
    imag_part = coefficients[..., 0, :] * gains[:, 1, :] + coefficients[..., 1, :] * gains[:, 0, :]
    return jnp.stack([real_part, imag_part], -2)


def mix_table(channel_mix):
    real_w = channel_mix[0]
    imag_w = channel_mix[1]
    return jnp.stack([jnp.stack([real_w, imag_w], 1), jnp.stack([-imag_w, real_w], 1)], 0)


def build_legendre(orders, log_sine, cosine, first_block, degrees, lat_total):
    slot_count = orders.shape[0]
    log_seeds = seed_logs(orders, log_sine)
    zero_state = jnp.zeros((slot_count, lat_total), jnp.float32)
    empty_table = jnp.zeros((slot_count, degrees, lat_total), jnp.bfloat16)

    def build_advance_block(block_index, carried):
        recursion, legendre = carried
        recursion, block_rows = legendre_rows(
            recursion, orders, log_seeds, block_index * LB, LB, cosine
        )
        legendre = lax.dynamic_update_slice_in_dim(
            legendre, block_rows.astype(jnp.bfloat16), block_index * LB, 1
        )
        return (recursion, legendre)

    start_carry = ((zero_state, zero_state, zero_state), empty_table)
    return lax.fori_loop(first_block, degrees // LB, build_advance_block, start_carry)[1]


def analyse_rows(legendre, fourier_part, first_block, degrees):
    slot_count = legendre.shape[0]
    channel_count = fourier_part.shape[3]
    empty_sum = jnp.zeros((slot_count, degrees, 2, channel_count), jnp.float32)

    def analyse_advance_block(block_index, summed):
        block_rows = lax.dynamic_slice_in_dim(legendre, block_index * LB, LB, 1)
        partial_sum = jnp.einsum(
            "glj,gjtc->gltc", block_rows, fourier_part, preferred_element_type=jnp.float32
        )
        return lax.dynamic_update_slice_in_dim(summed, partial_sum, block_index * LB, 1)

    return lax.fori_loop(first_block, degrees // LB, analyse_advance_block, empty_sum)


def synthesise_rows(legendre, mixed_part, first_block, degrees):
    slot_count, _, lat_total = legendre.shape
    channel_count = mixed_part.shape[3]
    empty_sum = jnp.zeros((slot_count, lat_total, 2, channel_count), jnp.float32)

    def synthesise_advance_block(block_index, summed):
        block_rows = lax.dynamic_slice_in_dim(legendre, block_index * LB, LB, 1)
        block_values = lax.dynamic_slice_in_dim(mixed_part, block_index * LB, LB, 1)
        return summed + jnp.einsum(
            "glj,gltc->gjtc", block_rows, block_values, preferred_element_type=jnp.float32
        )

    return lax.fori_loop(first_block, degrees // LB, synthesise_advance_block, empty_sum)


def on_device(signal, spectral_filter, channel_mix):
    lat_count = lax.axis_size("lat")
    chan_count = lax.axis_size("chan")
    lat_rows, quarter, lon_count = signal.shape
    lat_total = lat_rows * lat_count
    degrees = spectral_filter.shape[0]
    full_channels = channel_mix.shape[1]
    per_dev = degrees // lat_count
    sub_count = per_dev // chan_count
    lat_index = lax.axis_index("lat")
    chan_index = lax.axis_index("chan")
    every_slot = jnp.arange(degrees, dtype=jnp.int32)
    dest_dev = every_slot // per_dev
    slot_index = every_slot % per_dev
    own_slots = chan_index * sub_count + jnp.arange(sub_count, dtype=jnp.int32)
    orders_all = dest_dev * per_dev + slot_index
    orders_own = lat_index * per_dev + own_slots
    trig, synth = fourier_tables(orders_all, lon_count)
    own_rows = lat_index * lat_rows + jnp.arange(lat_rows, dtype=jnp.int32)
    _, _, own_weight = latitude_terms(own_rows, lat_total, lon_count)
    spectrum = jnp.einsum("acn,tkn->katc", signal, trig, preferred_element_type=jnp.float32)
    spectrum = (spectrum * own_weight[None, :, None, None]).astype(jnp.bfloat16)
    fourier = lax.all_to_all(
        lax.all_to_all(spectrum, "lat", split_axis=0, concat_axis=1, tiled=True),
        "chan",
        split_axis=0,
        concat_axis=3,
        tiled=True,
    )
    cosine, log_sine, _ = latitude_terms(
        jnp.arange(lat_total, dtype=jnp.int32), lat_total, lon_count
    )
    slot_total = orders_own.shape[0]
    first_end = slot_total // 2
    bounds = [(0, first_end), (first_end, slot_total)]
    tables = []
    first_blocks = []
    filtered_parts = []
    for start_slot, end_slot in bounds:
        group_orders = orders_own[start_slot:end_slot]
        first_block = jnp.min(group_orders) // LB
        legendre = build_legendre(group_orders, log_sine, cosine, first_block, degrees, lat_total)
        fourier_part = fourier[start_slot:end_slot]
        coefficients = analyse_rows(legendre, fourier_part, first_block, degrees)
        filtered_parts.append(apply_filter(coefficients, spectral_filter).astype(jnp.bfloat16))
        tables.append(legendre)
        first_blocks.append(first_block)
    filtered = jnp.concatenate(filtered_parts, 0)
    kernel = mix_table(channel_mix)
    flat_kernel = kernel.reshape(2 * full_channels, 2 * full_channels)
    mixed = jnp.dot(
        filtered.reshape(slot_total * degrees, 2 * full_channels),
        flat_kernel,
        preferred_element_type=jnp.float32,
    )
    mixed = mixed.astype(jnp.bfloat16).reshape(slot_total, degrees, 2, full_channels)
    back_parts = []
    for group_index in range(len(bounds)):
        start_slot, end_slot = bounds[group_index]
        mixed_part = mixed[start_slot:end_slot]
        back_parts.append(
            synthesise_rows(tables[group_index], mixed_part, first_blocks[group_index], degrees)
        )
    back = jnp.concatenate(back_parts, 0).astype(jnp.bfloat16)
    back = lax.all_to_all(back, "chan", split_axis=3, concat_axis=0, tiled=True)
    returned = lax.all_to_all(back, "lat", split_axis=1, concat_axis=0, tiled=True)
    output = jnp.einsum("katc,tkn->acn", returned, synth, preferred_element_type=jnp.float32)
    return output.astype(jnp.bfloat16)


def solution(mesh):
    return jax.shard_map(
        on_device,
        mesh=mesh,
        in_specs=(P("lat", "chan", None), P(), P()),
        out_specs=P("lat", "chan", None),
        check_vma=False,
    )
```

profile of v0, /device:TPU:0, one launch (start us, length us, event | category | flops | bytes accessed | tf_op | source)
XLA Modules:
  0.0 1342.0 jit_solution(16196962002320569169)
XLA Ops:
  0.0 10.2 fusion.40
  10.3 17.6 %fusion.27 = bf16[384,48,2,96]{0,3,1,2:T(8,128)(2,1)} fusion(f32[48]{0:T(128)S(1)} %sine_multiply_fusion, bf16[48,96,1440]{2,1,0:T(8,128)(2,1)} %param.19, f32[1,384,1440]{1,2,0:T(8,128)} %get-tuple-element.1470, f32[1,384,1440]{1,2,0:T(8,128)S(1)} %get-tuple-element.1469), kind=kOutput, calls=%fused_computation.192 | convolution fusion | flops 10203660288 | bytes 24772800 | tf_op jit(solution)/shard_map/acn,tkn->katc/dot_general | solution.py:145
  27.9 11.8 copy.33
  39.7 5.2 all-to-all-start
  48.7 331.1 %while.159 = (s32[]{:T(128)}, f32[6,384]{1,0:T(8,128)S(1)}, f32[6,384]{1,0:T(8,128)S(1)}, f32[6,384]{1,0:T(8,128)S(1)}, bf16[6,384,384]{2,0,1:T(8,128)(2,1)S(1)}...) while((s32[]{:T(128)}, f32[6,384]{1,0:T(8,128)S(1)}, ...), condition=%wide.region_4.5_spmd.clone.clone, body=%wide.region_1.4_spmd.clone.clone.sunk | while | flops 430591 | bytes 2527546 | solution.py:92
  48.9 110.0 %while.162 = (s32[]{:T(128)}, f32[6,384]{1,0:T(8,128)S(1)}, f32[6,384]{1,0:T(8,128)S(1)}, f32[6,384]{1,0:T(8,128)S(1)}, bf16[16,8,6,384]{3,2,1,0:T(8,128)(2,1)S(...) while((s32[]{:T(128)}, f32[6,384]{1,0:T(8,128)S(1)}, ...), condition=%wide.region_3.3_spmd.clone, body=%wide.region_2.2_spmd.clone.sunk | while | flops 424441 | bytes 941511 | solution.py:59
  159.2 110.0 %while.162 = (s32[]{:T(128)}, f32[6,384]{1,0:T(8,128)S(1)}, f32[6,384]{1,0:T(8,128)S(1)}, f32[6,384]{1,0:T(8,128)S(1)}, bf16[16,8,6,384]{3,2,1,0:T(8,128)(2,1)S(...) while((s32[]{:T(128)}, f32[6,384]{1,0:T(8,128)S(1)}, ...), condition=%wide.region_3.3_spmd.clone, body=%wide.region_2.2_spmd.clone.sunk | while | flops 424441 | bytes 941511 | solution.py:59
  269.6 110.0 %while.162 = (s32[]{:T(128)}, f32[6,384]{1,0:T(8,128)S(1)}, f32[6,384]{1,0:T(8,128)S(1)}, f32[6,384]{1,0:T(8,128)S(1)}, bf16[16,8,6,384]{3,2,1,0:T(8,128)(2,1)S(...) while((s32[]{:T(128)}, f32[6,384]{1,0:T(8,128)S(1)}, ...), condition=%wide.region_3.3_spmd.clone, body=%wide.region_2.2_spmd.clone.sunk | while | flops 424441 | bytes 941511 | solution.py:59
  382.6 10.2 copy.34
  392.8 11.4 copy.35
  404.2 6.2 all-to-all-start.1
  410.7 320.8 %while.161 = (s32[]{:T(128)}, f32[6,384]{1,0:T(8,128)S(1)}, f32[6,384]{1,0:T(8,128)S(1)}, f32[6,384]{1,0:T(8,128)S(1)}, bf16[6,384,384]{2,0,1:T(8,128)(2,1)S(1)}...) while((s32[]{:T(128)}, f32[6,384]{1,0:T(8,128)S(1)}, ...), condition=%wide.region_11.12_spmd.clone.clone, body=%wide.region_8.11_spmd.clone.clone.sunk | while | flops 430591 | bytes 2527546 | solution.py:92
  411.0 106.5 %while.163 = (s32[]{:T(128)}, f32[6,384]{1,0:T(8,128)S(1)}, f32[6,384]{1,0:T(8,128)S(1)}, f32[6,384]{1,0:T(8,128)S(1)}, bf16[16,8,6,384]{3,2,1,0:T(8,128)(2,1)S(...) while((s32[]{:T(128)}, f32[6,384]{1,0:T(8,128)S(1)}, ...), condition=%wide.region_10.10_spmd.clone, body=%wide.region_9.9_spmd.clone.sunk | while | flops 424441 | bytes 941511 | solution.py:59
  517.9 106.5 %while.163 = (s32[]{:T(128)}, f32[6,384]{1,0:T(8,128)S(1)}, f32[6,384]{1,0:T(8,128)S(1)}, f32[6,384]{1,0:T(8,128)S(1)}, bf16[16,8,6,384]{3,2,1,0:T(8,128)(2,1)S(...) while((s32[]{:T(128)}, f32[6,384]{1,0:T(8,128)S(1)}, ...), condition=%wide.region_10.10_spmd.clone, body=%wide.region_9.9_spmd.clone.sunk | while | flops 424441 | bytes 941511 | solution.py:59
  624.8 106.5 %while.163 = (s32[]{:T(128)}, f32[6,384]{1,0:T(8,128)S(1)}, f32[6,384]{1,0:T(8,128)S(1)}, f32[6,384]{1,0:T(8,128)S(1)}, bf16[16,8,6,384]{3,2,1,0:T(8,128)(2,1)S(...) while((s32[]{:T(128)}, f32[6,384]{1,0:T(8,128)S(1)}, ...), condition=%wide.region_10.10_spmd.clone, body=%wide.region_9.9_spmd.clone.sunk | while | flops 424441 | bytes 941511 | solution.py:59
  734.7 4.2 copy.46
  747.9 5.9 fusion.71
  756.1 4.5 copy.38
  760.7 3.6 broadcast.1824.clone.1
  764.3 9.8 while.154
  774.1 4.3 copy.41
  778.3 4.5 copy.43
  786.4 10.0 while.155
  796.4 6.5 subtract_convert_fusion.1
  803.9 68.3 %copy.44 = bf16[12,384,2,384]{3,2,1,0:T(2,128)(2,1)S(1)} copy(bf16[12,384,2,384]{3,1,2,0:T(8,128)(2,1)S(1)} %maximum_maximum_fusion) | data formatting | bytes 14155776 | tf_op jit(solution)/shard_map/concatenate | solution.py:172
  873.4 7.2 convolution_convert_fusion
  884.0 6.6 slice.191
  890.6 3.6 broadcast.1824.clone.3
  894.3 24.2 %while.156 = (s32[]{:T(128)}, f32[6,384,2,384]{3,1,2,0:T(8,128)}, bf16[6,384,384]{1,2,0:T(8,128)(2,1)}, bf16[6,384,2,384]{3,2,1,0:T(2,128)(2,1)S(1)}, s32[]{:T(128)}, /*index=5*/s32[]{:T(128)}, s32[]{:T(128)}, s32[]{:T(128)}) while((s32[]{:T(128)}, f32[6,384,2,384]{3,1,2,0:T(8,128)}, bf16[6,384,384]{1,2,0:T(8,128)(2,1)}, ...), condition=%wide.region_15.16_spmd, body=%wide.region_14.15_spmd.sunk | while | flops 454754304 | bytes 18284684 | solution.py:122
  895.1 7.3 convolution_add_fusion.4
  903.2 7.3 convolution_add_fusion.4
  911.2 7.3 convolution_add_fusion.4
  918.5 12.9 copy.48
  931.4 6.6 slice.193
  941.6 24.6 %while.157 = (s32[]{:T(128)}, f32[6,384,2,384]{3,1,2,0:T(8,128)}, bf16[6,384,384]{1,2,0:T(8,128)(2,1)}, bf16[6,384,2,384]{3,2,1,0:T(2,128)(2,1)S(1)}, s32[]{:T(128)}, /*index=5*/s32[]{:T(128)}, s32[]{:T(128)}, s32[]{:T(128)}) while((s32[]{:T(128)}, f32[6,384,2,384]{3,1,2,0:T(8,128)}, bf16[6,384,384]{1,2,0:T(8,128)(2,1)}, ...), condition=%wide.region_17.18_spmd, body=%wide.region_16.17_spmd.sunk | while | flops 454754304 | bytes 18284684 | solution.py:122
  942.9 7.3 convolution_add_fusion.5
  950.9 7.3 convolution_add_fusion.5
  959.0 7.3 convolution_add_fusion.5
  966.3 13.1 copy.51
  979.4 18.3 %pad_maximum_fusion = bf16[12,384,2,384]{1,2,0,3:T(2,128)(2,1)S(1)} fusion(bf16[6,384,2,384]{1,2,0,3:T(2,128)(2,1)} %copy.51, bf16[6,384,2,384]{1,2,0,3:T(2,128)(2,1)S(1)} %copy-done.1), kind=kLoop, calls=%fused_computation.194 | loop fusion | flops 3538944 | bytes 14155776 | tf_op jit(solution)/shard_map/concatenate | solution.py:188
  997.7 160.6 %all_to_all.69 = bf16[12,384,2,384]{1,2,0,3:T(2,128)(2,1)S(1)} all-to-all(bf16[12,384,2,384]{1,2,0,3:T(2,128)(2,1)S(1)} %pad_maximum_fusion), channel_id=1, replica_groups=mesh['lat'=8,'chan'=4] {'chan'}, dimensions={3} | all-to-all | bytes 14155776 | tf_op jit(solution)/shard_map/all_to_all | solution.py:189
  1159.6 4.3 copy.53
  1163.9 20.6 %copy.54 = bf16[48,384,2,96]{3,2,0,1:T(2,128)(2,1)} copy(bf16[48,384,2,96]{1,3,2,0:T(8,128)(2,1)} %bitcast.405) | data formatting | bytes 14155776 | tf_op jit(solution)/shard_map/all_to_all | solution.py:189
  1184.5 5.1 all-to-all-start.3
  1189.5 105.3 %all-to-all-done.3 = bf16[48,384,2,96]{3,2,0,1:T(2,128)(2,1)} async-done(((bf16[48,384,2,96]{3,2,0,1:T(2,128)(2,1)}), bf16[48,384,2,96]{3,2,0,1:T(2,128)(2,1)}, u32[]{:S(2)}, u32[]{:S(2)}) %all-to-all-start.3) | async-done | bytes 7077920 | tf_op jit(solution)/shard_map/all_to_all | solution.py:190
  1294.8 11.1 copy.55
  1305.9 9.3 copy.56
  1315.2 26.6 %bitcast_convert_fusion = bf16[48,96,1440]{2,1,0:T(8,128)(2,1)} fusion(bf16[384,48,2,96]{3,1,2,0:T(8,128)(2,1)} %bitcast.410, f32[1,384,1440]{1,2,0:T(8,128)} %get-tuple-element.1470, f32[1,384,1440]{1,2,0:T(8,128)S(1)} %copy-done.3, f32[384]{0:T(512)S(1)} %compare_select_fusion.4), kind=kOutput, calls=%fused_computation.186 | convolution fusion | flops 10202112000 | bytes 24774144 | tf_op jit(solution)/shard_map/katc,tkn->acn/dot_general | solution.py:191
  (1529 shorter events, 220.6 us)
Async XLA Ops:
  10.2 17.7 %copy-start.2 = (f32[1,384,1440]{1,2,0:T(8,128)}, f32[1,384,1440]{1,2,0:T(8,128)S(1)}, u32[]{:S(2)}) copy-start(f32[1,384,1440]{1,2,0:T(8,128)S(1)} %get-tuple-element.1469) | copy-start | bytes 6635524
  39.7 342.9 %all-to-all-start = ((bf16[384,48,2,96]{3,1,2,0:T(8,128)(2,1)}), bf16[384,48,2,96]{3,1,2,0:T(8,128)(2,1)}, u32[]{:S(2)}, u32[]{:S(2)}) async-start(bf16[384,48,2,96]{3,1,2,0:T(8,128)(2,1)} %copy.33), calls=%async_computation | async-start | bytes 18874368 | tf_op jit(solution)/shard_map/all_to_all | solution.py:148
  379.8 13.1 copy-start
  404.2 343.6 %all-to-all-start.1 = ((bf16[48,384,2,96]{1,3,2,0:T(8,128)(2,1)}), bf16[48,384,2,96]{1,3,2,0:T(8,128)(2,1)}, u32[]{:S(2)}, u32[]{:S(2)}) async-start(bf16[48,384,2,96]{1,3,2,0:T(8,128)(2,1)} %copy.35), calls=%async_computation.1 | async-start | bytes 14155776 | tf_op jit(solution)/shard_map/all_to_all | solution.py:147
  738.9 4.1 copy-start.4
  743.2 2.6 copy-start.5
  966.3 13.1 copy-start.1
  1184.5 110.4 %all-to-all-start.3 = ((bf16[48,384,2,96]{3,2,0,1:T(2,128)(2,1)}), bf16[48,384,2,96]{3,2,0,1:T(2,128)(2,1)}, u32[]{:S(2)}, u32[]{:S(2)}) async-start(bf16[48,384,2,96]{3,2,0,1:T(2,128)(2,1)} %copy.54), calls=%async_computation.3 | async-start | bytes 18874368 | tf_op jit(solution)/shard_map/all_to_all | solution.py:190
  1305.9 9.3 copy-start.3
where the time goes:
time: 1360 us; the launch traced here: 1340 us
  loops' own time  486 us (36%)
  local copies, waits for them, and re-layouts  318 us (23%)
  blocking collectives  161 us (12%)
  other arithmetic  135 us (10%)
  matrix products  114 us (8%)
  waiting for transfers between devices  105 us (8%)
  starting transfers between devices  16.5 us (1%)
    another operation x6, loops' own time, legendre_rows(): carried, values = lax.scan(advance, recursion, degrees_here, unroll=8)  485 us
    all_to_all x1, blocking collectives, on_device(): back = lax.all_to_all(back, 'chan', split_axis=3, concat_axis=0, tiled=True)  161 us
    all_to_all x1, waiting for transfers between devices, on_device(): lax.all_to_all(back, 'lat', split_axis=1, concat_axis=0, tiled=True)  105 us
    while x672, other arithmetic  68.7 us
    concatenate x1, local copies, waits for them, and re-layouts, on_device(): filtered = jnp.concatenate(filtered_parts, 0)  68.3 us
    slice x96, local copies, waits for them, and re-layouts, legendre_rows(): carried, values = lax.scan(advance, recursion, degrees_here, unroll=8)  58.7 us
    dot_general x6, matrix products, synthesise_advance_block(): jnp.einsum('glj,gltc->gjtc', block_rows, block_values, preferred_element_...  43.5 us
    while x4, local copies, waits for them, and re-layouts, synthesise_rows(): lax.fori_loop(first_block, degrees // LB, synthesise_advance_block, empty...  32.8 us
  transfers between devices with their start and end apart: 3, of which 1 were waited for; matrix products, arithmetic and copies ran while one was open for 14% of the time, Pallas kernels for 0%

commit v1 on v0

--- a/solution.py
+++ b/solution.py
@@ -144,13 +144,19 @@
     _, _, own_weight = latitude_terms(own_rows, lat_total, lon_count)
     spectrum = jnp.einsum("acn,tkn->katc", signal, trig, preferred_element_type=jnp.float32)
     spectrum = (spectrum * own_weight[None, :, None, None]).astype(jnp.bfloat16)
-    fourier = lax.all_to_all(
-        lax.all_to_all(spectrum, "lat", split_axis=0, concat_axis=1, tiled=True),
-        "chan",
-        split_axis=0,
-        concat_axis=3,
-        tiled=True,
-    )
+    x = lax.all_to_all(spectrum, "lat", split_axis=0, concat_axis=1, tiled=True)
+    ways, here = (lax.axis_size("chan"), lax.axis_index("chan"))
+    width = x.shape[0] // ways
+    shape = list(x.shape)
+    shape[0] = width
+    height = shape[3]
+    shape[3] = height * ways
+    fourier = jnp.zeros(shape, x.dtype)
+    for mask in range(ways):
+        part = lax.dynamic_slice_in_dim(x, (here ^ mask) * width, width, axis=0)
+        if mask:
+            part = lax.ppermute(part, "chan", [(d, d ^ mask) for d in range(ways)])
+        fourier = lax.dynamic_update_slice_in_dim(fourier, part, (here ^ mask) * height, axis=3)
     cosine, log_sine, _ = latitude_terms(
         jnp.arange(lat_total, dtype=jnp.int32), lat_total, lon_count
     )

time: 1360 us -> 1450 us (1.066)
  local copies, waits for them, and re-layouts: 318 us -> 401 us
    dynamic_update_slice x0 -> x4, local copies, waits for them, and re-layouts: none -> 73.2 us  [on_device(): lax.dynamic_update_slice_in_dim(fourier, part, (here ^ mask) * height, ax...]
    dynamic_slice x0 -> x4, local copies, waits for them, and re-layouts: none -> 19.9 us  [on_device(): part = lax.dynamic_slice_in_dim(x, (here ^ mask) * width, width, axis=0)]
  transfers between devices with their start and end apart: 3 -> 5, of which waited for: 1 -> 1; matrix products, arithmetic and copies ran while one was open for 14% -> 18% of each run, Pallas kernels for 0% -> 0%
where the time goes in v1:
time: 1450 us; the launch traced here: 1430 us
  loops' own time  494 us (34%)
  local copies, waits for them, and re-layouts  401 us (28%)
  blocking collectives  159 us (11%)
  other arithmetic  135 us (9%)
  matrix products  118 us (8%)
  waiting for transfers between devices  105 us (7%)
  starting transfers between devices  15.8 us (1%)
    another operation x6, loops' own time, legendre_rows(): carried, values = lax.scan(advance, recursion, degrees_here, unroll=8)  485 us
    all_to_all x1, blocking collectives, on_device(): back = lax.all_to_all(back, 'chan', split_axis=3, concat_axis=0, tiled=True)  159 us
    all_to_all x1, waiting for transfers between devices, on_device(): lax.all_to_all(back, 'lat', split_axis=1, concat_axis=0, tiled=True)  105 us
    dynamic_update_slice x4, local copies, waits for them, and re-layouts, on_device(): lax.dynamic_update_slice_in_dim(fourier, part, (here ^ mask) * height, ax...  73.2 us
    while x672, other arithmetic  68.7 us
    concatenate x1, local copies, waits for them, and re-layouts, on_device(): filtered = jnp.concatenate(filtered_parts, 0)  68.3 us
    slice x96, local copies, waits for them, and re-layouts, legendre_rows(): carried, values = lax.scan(advance, recursion, degrees_here, unroll=8)  59.1 us
    dot_general x6, matrix products, synthesise_advance_block(): jnp.einsum('glj,gltc->gjtc', block_rows, block_values, preferred_element_...  43.5 us
  transfers between devices with their start and end apart: 5, of which 1 were waited for; matrix products, arithmetic and copies ran while one was open for 18% of the time, Pallas kernels for 0%

profile of v1, /device:TPU:0, one launch (start us, length us, event | category | flops | bytes accessed | tf_op | source)
XLA Modules:
  0.0 1434.6 jit_solution(6373741635568239589)
XLA Ops:
  0.0 10.2 fusion.40
  10.3 17.6 %fusion.27 = bf16[384,48,2,96]{0,3,1,2:T(8,128)(2,1)} fusion(f32[48]{0:T(128)S(1)} %sine_multiply_fusion, bf16[48,96,1440]{2,1,0:T(8,128)(2,1)} %param.19, f32[1,384,1440]{1,2,0:T(8,128)} %get-tuple-element.1490, f32[1,384,1440]{1,2,0:T(8,128)S(1)} %get-tuple-element.1489), kind=kOutput, calls=%fused_computation.192 | convolution fusion | flops 10203660288 | bytes 24772800 | tf_op jit(solution)/shard_map/acn,tkn->katc/dot_general | solution.py:145
  27.9 11.8 copy.46
  39.7 5.2 all-to-all-start
  48.6 329.8 %while.161 = (s32[]{:T(128)}, f32[6,384]{1,0:T(8,128)S(1)}, f32[6,384]{1,0:T(8,128)S(1)}, f32[6,384]{1,0:T(8,128)S(1)}, bf16[6,384,384]{2,0,1:T(8,128)(2,1)S(1)}...) while((s32[]{:T(128)}, f32[6,384]{1,0:T(8,128)S(1)}, ...), condition=%wide.region_11.12_spmd.clone.clone, body=%wide.region_8.11_spmd.clone.clone.sunk | while | flops 430591 | bytes 2527546 | solution.py:92
  48.8 109.5 %while.163 = (s32[]{:T(128)}, f32[6,384]{1,0:T(8,128)S(1)}, f32[6,384]{1,0:T(8,128)S(1)}, f32[6,384]{1,0:T(8,128)S(1)}, bf16[16,8,6,384]{3,2,1,0:T(8,128)(2,1)S(...) while((s32[]{:T(128)}, f32[6,384]{1,0:T(8,128)S(1)}, ...), condition=%wide.region_10.10_spmd.clone, body=%wide.region_9.9_spmd.clone.sunk | while | flops 424441 | bytes 941511 | solution.py:59
  158.6 109.5 %while.163 = (s32[]{:T(128)}, f32[6,384]{1,0:T(8,128)S(1)}, f32[6,384]{1,0:T(8,128)S(1)}, f32[6,384]{1,0:T(8,128)S(1)}, bf16[16,8,6,384]{3,2,1,0:T(8,128)(2,1)S(...) while((s32[]{:T(128)}, f32[6,384]{1,0:T(8,128)S(1)}, ...), condition=%wide.region_10.10_spmd.clone, body=%wide.region_9.9_spmd.clone.sunk | while | flops 424441 | bytes 941511 | solution.py:59
  268.5 109.5 %while.163 = (s32[]{:T(128)}, f32[6,384]{1,0:T(8,128)S(1)}, f32[6,384]{1,0:T(8,128)S(1)}, f32[6,384]{1,0:T(8,128)S(1)}, bf16[16,8,6,384]{3,2,1,0:T(8,128)(2,1)S(...) while((s32[]{:T(128)}, f32[6,384]{1,0:T(8,128)S(1)}, ...), condition=%wide.region_10.10_spmd.clone, body=%wide.region_9.9_spmd.clone.sunk | while | flops 424441 | bytes 941511 | solution.py:59
  381.0 10.2 copy.47
  391.3 7.7 constant_dynamic-slice_fusion.4
  418.4 324.8 %while.159 = (s32[]{:T(128)}, f32[6,384]{1,0:T(8,128)S(1)}, f32[6,384]{1,0:T(8,128)S(1)}, f32[6,384]{1,0:T(8,128)S(1)}, bf16[6,384,384]{2,0,1:T(8,128)(2,1)}, /*...) while((s32[]{:T(128)}, f32[6,384]{1,0:T(8,128)S(1)}, ...), condition=%wide.region_4.5_spmd.clone.clone, body=%wide.region_1.4_spmd.clone.clone.sunk | while | flops 430591 | bytes 2330938 | solution.py:92
  418.6 107.1 %while.162 = (s32[]{:T(128)}, f32[6,384]{1,0:T(8,128)S(1)}, f32[6,384]{1,0:T(8,128)S(1)}, f32[6,384]{1,0:T(8,128)S(1)}, bf16[16,8,6,384]{3,2,1,0:T(8,128)(2,1)S(...) while((s32[]{:T(128)}, f32[6,384]{1,0:T(8,128)S(1)}, ...), condition=%wide.region_3.3_spmd.clone, body=%wide.region_2.2_spmd.clone.sunk | while | flops 424441 | bytes 941511 | solution.py:59
  526.8 107.1 %while.162 = (s32[]{:T(128)}, f32[6,384]{1,0:T(8,128)S(1)}, f32[6,384]{1,0:T(8,128)S(1)}, f32[6,384]{1,0:T(8,128)S(1)}, bf16[16,8,6,384]{3,2,1,0:T(8,128)(2,1)S(...) while((s32[]{:T(128)}, f32[6,384]{1,0:T(8,128)S(1)}, ...), condition=%wide.region_3.3_spmd.clone, body=%wide.region_2.2_spmd.clone.sunk | while | flops 424441 | bytes 941511 | solution.py:59
  635.1 107.1 %while.162 = (s32[]{:T(128)}, f32[6,384]{1,0:T(8,128)S(1)}, f32[6,384]{1,0:T(8,128)S(1)}, f32[6,384]{1,0:T(8,128)S(1)}, bf16[16,8,6,384]{3,2,1,0:T(8,128)(2,1)S(...) while((s32[]{:T(128)}, f32[6,384]{1,0:T(8,128)S(1)}, ...), condition=%wide.region_3.3_spmd.clone, body=%wide.region_2.2_spmd.clone.sunk | while | flops 424441 | bytes 941511 | solution.py:59
  763.7 15.4 %dynamic_update_slice.47 = bf16[12,384,2,384]{3,1,2,0:T(8,128)(2,1)} dynamic-update-slice(bf16[12,384,2,384]{3,1,2,0:T(8,128)(2,1)} %broadcast_in_dim.705, bf16[12,384,2,96]{3,1,2,0:T(8,128)(2,1)S(1)} %copy-done.1, s32[]{:T(128)} %constant.384.clone.1, s32[]{:T(128)} %constant.384.clone.1, s32[]{:T(128)} %constant.384.clone.1, s32[]{:T(128)S(6)} %select_n.518) | dynamic-update-slice | bytes 3538948 | tf_op jit(solution)/shard_map/dynamic_update_slice | solution.py:159
  782.0 19.5 %dynamic_update_slice.48 = bf16[12,384,2,384]{3,1,2,0:T(8,128)(2,1)} dynamic-update-slice(bf16[12,384,2,384]{3,1,2,0:T(8,128)(2,1)} %dynamic_update_slice.47, bf16[12,384,2,96]{3,1,2,0:T(8,128)(2,1)S(1)} %copy.49, s32[]{:T(128)} %constant.384.clone.1, s32[]{:T(128)} %constant.384.clone.1, s32[]{:T(128)} %constant.384.clone.1, s32[]{:T(128)S(6)} %select_n.520) | dynamic-update-slice | bytes 3538948 | tf_op jit(solution)/shard_map/dynamic_update_slice | solution.py:159
  804.4 19.5 %dynamic_update_slice.49 = bf16[12,384,2,384]{3,1,2,0:T(8,128)(2,1)} dynamic-update-slice(bf16[12,384,2,384]{3,1,2,0:T(8,128)(2,1)} %dynamic_update_slice.48, bf16[12,384,2,96]{3,1,2,0:T(8,128)(2,1)S(1)} %copy.51, s32[]{:T(128)} %constant.384.clone.1, s32[]{:T(128)} %constant.384.clone.1, s32[]{:T(128)} %constant.384.clone.1, s32[]{:T(128)S(6)} %select_n.522) | dynamic-update-slice | bytes 3538948 | tf_op jit(solution)/shard_map/dynamic_update_slice | solution.py:159
  826.9 18.7 %dynamic_update_slice.50 = bf16[12,384,2,384]{3,1,2,0:T(8,128)(2,1)} dynamic-update-slice(bf16[12,384,2,384]{3,1,2,0:T(8,128)(2,1)} %dynamic_update_slice.49, bf16[12,384,2,96]{3,1,2,0:T(8,128)(2,1)S(1)} %copy.53, s32[]{:T(128)} %constant.384.clone.1, s32[]{:T(128)} %constant.384.clone.1, s32[]{:T(128)} %constant.384.clone.1, s32[]{:T(128)S(6)} %select_n.524) | dynamic-update-slice | bytes 3538948 | tf_op jit(solution)/shard_map/dynamic_update_slice | solution.py:159
  845.6 5.8 fusion.71
  854.9 13.2 while.155
  854.9 4.4 convolution_dynamic-update-slice_fusion.5
  859.3 4.4 convolution_dynamic-update-slice_fusion.5
  863.7 4.4 convolution_dynamic-update-slice_fusion.5
  871.8 18.1 %while.154 = (s32[]{:T(128)}, f32[6,384,2,384]{3,1,2,0:T(8,128)}, bf16[6,384,384]{2,1,0:T(8,128)(2,1)}, bf16[6,384,2,384]{3,1,2,0:T(8,128)(2,1)S(1)}, s32[]{:T(128)}, /*index=5*/s32[]{:T(128)}, s32[]{:T(128)}, s32[]{:T(128)}) while((s32[]{:T(128)}, f32[6,384,2,384]{3,1,2,0:T(8,128)}, bf16[6,384,384]{2,1,0:T(8,128)(2,1)}, ...), condition=%wide.region_6.7_spmd, body=%wide.region_5.6_spmd.sunk | while | flops 452984832 | bytes 6489219 | solution.py:107
  889.9 6.5 subtract_convert_fusion.1
  897.5 68.3 %copy.58 = bf16[12,384,2,384]{3,2,1,0:T(2,128)(2,1)S(1)} copy(bf16[12,384,2,384]{3,1,2,0:T(8,128)(2,1)S(1)} %maximum_maximum_fusion) | data formatting | bytes 14155776 | tf_op jit(solution)/shard_map/concatenate | solution.py:178
  967.0 7.2 convolution_convert_fusion
  977.5 6.6 slice.183
  987.8 24.2 %while.156 = (s32[]{:T(128)}, f32[6,384,2,384]{3,1,2,0:T(8,128)}, bf16[6,384,384]{1,2,0:T(8,128)(2,1)}, bf16[6,384,2,384]{3,2,1,0:T(2,128)(2,1)S(1)}, s32[]{:T(128)}, /*index=5*/s32[]{:T(128)}, s32[]{:T(128)}, s32[]{:T(128)}) while((s32[]{:T(128)}, f32[6,384,2,384]{3,1,2,0:T(8,128)}, bf16[6,384,384]{1,2,0:T(8,128)(2,1)}, ...), condition=%wide.region_15.16_spmd, body=%wide.region_14.15_spmd.sunk | while | flops 454754304 | bytes 18284684 | solution.py:122
  988.6 7.3 convolution_add_fusion.4
  996.7 7.3 convolution_add_fusion.4
  1004.7 7.3 convolution_add_fusion.4
  1012.0 12.9 copy.62
  1024.9 6.6 slice.185
  1035.2 24.4 %while.157 = (s32[]{:T(128)}, f32[6,384,2,384]{3,1,2,0:T(8,128)}, bf16[6,384,384]{1,2,0:T(8,128)(2,1)}, bf16[6,384,2,384]{3,2,1,0:T(2,128)(2,1)S(1)}, s32[]{:T(128)}, /*index=5*/s32[]{:T(128)}, s32[]{:T(128)}, s32[]{:T(128)}) while((s32[]{:T(128)}, f32[6,384,2,384]{3,1,2,0:T(8,128)}, bf16[6,384,384]{1,2,0:T(8,128)(2,1)}, ...), condition=%wide.region_17.18_spmd, body=%wide.region_16.17_spmd.sunk | while | flops 454754304 | bytes 18284684 | solution.py:122
  1036.2 7.3 convolution_add_fusion.5
  1044.3 7.3 convolution_add_fusion.5
  1052.3 7.3 convolution_add_fusion.5
  1059.6 13.1 copy.65
  1072.7 18.3 %pad_maximum_fusion = bf16[12,384,2,384]{1,2,0,3:T(2,128)(2,1)S(1)} fusion(bf16[6,384,2,384]{1,2,0,3:T(2,128)(2,1)} %copy.65, bf16[6,384,2,384]{1,2,0,3:T(2,128)(2,1)S(1)} %copy-done), kind=kLoop, calls=%fused_computation.194 | loop fusion | flops 3538944 | bytes 14155776 | tf_op jit(solution)/shard_map/concatenate | solution.py:194
  1091.0 159.5 %all_to_all.54 = bf16[12,384,2,384]{1,2,0,3:T(2,128)(2,1)S(1)} all-to-all(bf16[12,384,2,384]{1,2,0,3:T(2,128)(2,1)S(1)} %pad_maximum_fusion), channel_id=1, replica_groups=mesh['lat'=8,'chan'=4] {'chan'}, dimensions={3} | all-to-all | bytes 14155776 | tf_op jit(solution)/shard_map/all_to_all | solution.py:195
  1251.8 4.3 copy.67
  1256.1 20.6 %copy.68 = bf16[48,384,2,96]{3,2,0,1:T(2,128)(2,1)} copy(bf16[48,384,2,96]{1,3,2,0:T(8,128)(2,1)} %bitcast.400) | data formatting | bytes 14155776 | tf_op jit(solution)/shard_map/all_to_all | solution.py:195
  1276.7 5.1 all-to-all-start.2
  1281.8 105.3 %all-to-all-done.2 = bf16[48,384,2,96]{3,2,0,1:T(2,128)(2,1)} async-done(((bf16[48,384,2,96]{3,2,0,1:T(2,128)(2,1)}), bf16[48,384,2,96]{3,2,0,1:T(2,128)(2,1)}, u32[]{:S(2)}, u32[]{:S(2)}) %all-to-all-start.2) | async-done | bytes 7077920 | tf_op jit(solution)/shard_map/all_to_all | solution.py:196
  1387.1 11.1 copy.69
  1398.1 9.3 copy.70
  1407.5 26.7 %bitcast_convert_fusion = bf16[48,96,1440]{2,1,0:T(8,128)(2,1)} fusion(bf16[384,48,2,96]{3,1,2,0:T(8,128)(2,1)} %bitcast.403, f32[1,384,1440]{1,2,0:T(8,128)} %get-tuple-element.1490, f32[1,384,1440]{1,2,0:T(8,128)S(1)} %copy-done.3, f32[384]{0:T(512)S(1)} %compare_select_fusion.4), kind=kOutput, calls=%fused_computation.186 | convolution fusion | flops 10202112000 | bytes 24774144 | tf_op jit(solution)/shard_map/katc,tkn->acn/dot_general | solution.py:197
  (1540 shorter events, 254.9 us)
Async XLA Ops:
  10.2 17.7 %copy-start.2 = (f32[1,384,1440]{1,2,0:T(8,128)}, f32[1,384,1440]{1,2,0:T(8,128)S(1)}, u32[]{:S(2)}) copy-start(f32[1,384,1440]{1,2,0:T(8,128)S(1)} %get-tuple-element.1489) | copy-start | bytes 6635524
  39.7 341.3 %all-to-all-start = ((bf16[384,48,2,96]{3,1,2,0:T(8,128)(2,1)}), bf16[384,48,2,96]{3,1,2,0:T(8,128)(2,1)}, u32[]{:S(2)}, u32[]{:S(2)}) async-start(bf16[384,48,2,96]{3,1,2,0:T(8,128)(2,1)} %copy.46), calls=%async_computation | async-start | bytes 18874368 | tf_op jit(solution)/shard_map/all_to_all | solution.py:147
  403.1 376.0 %collective-permute-start = (bf16[12,384,2,96]{1,3,2,0:T(8,128)(2,1)}, bf16[12,384,2,96]{1,3,2,0:T(8,128)(2,1)}, u32[]{:S(2)}, u32[]{:S(2)}) collective-permute-start(bf16[12,384,2,96]{1,3,2,0:T(8,128)(2,1)} %copy.48), channel_id=1, source_target_pairs={{0,1},{1,0},{2,3},{3,2},{4,5},{5,4},{6,7},{7,6},{8,9},{9,8},{10,11... | collective-permute-start | bytes 5308424 | tf_op jit(solution)/shard_map/ppermute | solution.py:158
  410.1 391.4 %collective-permute-start.1 = (bf16[12,384,2,96]{1,3,2,0:T(8,128)(2,1)}, bf16[12,384,2,96]{1,3,2,0:T(8,128)(2,1)}, u32[]{:S(2)}, u32[]{:S(2)}) collective-permute-start(bf16[12,384,2,96]{1,3,2,0:T(8,128)(2,1)} %copy.50), channel_id=1, source_target_pairs={{0,2},{1,3},{2,0},{3,1},{4,6},{5,7},{6,4},{7,5},{8,10},{9,11},{10,... | collective-permute-start | bytes 5308424 | tf_op jit(solution)/shard_map/ppermute | solution.py:158
  416.8 407.2 %collective-permute-start.2 = (bf16[12,384,2,96]{1,3,2,0:T(8,128)(2,1)}, bf16[12,384,2,96]{1,3,2,0:T(8,128)(2,1)}, u32[]{:S(2)}, u32[]{:S(2)}) collective-permute-start(bf16[12,384,2,96]{1,3,2,0:T(8,128)(2,1)} %copy.52), channel_id=1, source_target_pairs={{0,3},{1,2},{2,1},{3,0},{4,7},{5,6},{6,5},{7,4},{8,11},{9,10},{10,... | collective-permute-start | bytes 5308424 | tf_op jit(solution)/shard_map/ppermute | solution.py:158
  750.5 4.2 copy-start.4
  754.9 2.6 copy-start.5
  759.7 4.0 copy-start.1
  1059.6 13.1 copy-start
  1276.7 110.4 %all-to-all-start.2 = ((bf16[48,384,2,96]{3,2,0,1:T(2,128)(2,1)}), bf16[48,384,2,96]{3,2,0,1:T(2,128)(2,1)}, u32[]{:S(2)}, u32[]{:S(2)}) async-start(bf16[48,384,2,96]{3,2,0,1:T(2,128)(2,1)} %copy.68), calls=%async_computation.2 | async-start | bytes 18874368 | tf_op jit(solution)/shard_map/all_to_all | solution.py:196
  1398.1 9.3 copy-start.3
